TPU v7x, 32 devices: a whole 2x2x4 slice. The times are simulated.
32 devices in a mesh: det: 8 (over y, x, core), row: 4 (over z).
Axes of the slice: x: 2, y: 2, z: 4, core: 2. Of those that a mesh axis runs over, the one named last changes fastest.
Arguments:
- coefficients: bfloat16 [8, 2048, 200], P('det', 'row'), may hold values from -1 to 1
- amplitudes: bfloat16 [8], P('det'), may hold values from -3 to 3
- plan: int32 [8, 2, 1], P('det'), may hold values 0 or 1
Outputs:
- density: float32 [2048, 2048], P('det', 'row')
All inputs are finite; a program needn't handle non-finite values. No bound on the sum of `plan` on one device may be relied on, other than what follows from the above.
Results may differ from a plain program's by a relative error of at most 0.0024.
Values may be sent and summed in bfloat16 or wider, within the bound.
A program may use at most 64 MiB of HBM per device.

v0:
```python
import jax
import jax.numpy as jnp
from jax import lax
from jax.sharding import PartitionSpec as P

ORDER = 2


def shifted(block, axis, distance):
    devices = range(lax.axis_size(axis))
    route = [((i - distance) % len(devices), i) for i in devices]
    return lax.ppermute(block, axis, route)


def neumann(correlation):
    identity = jnp.eye(correlation.shape[-1], dtype=jnp.float32)
    remainder = identity - correlation
    inverse = identity + jnp.zeros_like(correlation)
    for level in range(ORDER):
        inverse = identity + jnp.einsum(
            "...ab,...bc->...ac", remainder, inverse, precision=lax.Precision.HIGHEST
        )
    return inverse


def on_device(coefficients, amplitudes, plan):
    masks = plan.astype(jnp.float32)
    ket_amps = amplitudes.astype(jnp.float32)
    distances = plan.shape[1]
    ket_whole = lax.all_gather(coefficients, "row", axis=1, tiled=True)
    accum = jnp.zeros(
        (coefficients.shape[0], coefficients.shape[2], coefficients.shape[1]), jnp.float32
    )
    visitor = (coefficients, amplitudes)
    for step in range(distances):
        if step > 0:
            visitor = shifted((visitor[0], visitor[1]), "det", 1)
        visitor_full = lax.all_gather(visitor[0], "row", axis=1, tiled=True)
        correlation = jnp.einsum(
            "ina,jnb->ijab", visitor_full, ket_whole, preferred_element_type=jnp.float32
        )
        weight = visitor[1].astype(jnp.float32)[:, None] * ket_amps[None, :] * masks[:, step, :].T
        scaled = (weight[:, :, None, None] * neumann(correlation)).astype(jnp.bfloat16)
        accum = accum + jnp.einsum(
            "ijba,ina->jbn", scaled, visitor[0], preferred_element_type=jnp.float32
        )
    folded = accum.astype(jnp.bfloat16)
    return lax.psum_scatter(
        jnp.einsum("jmb,jbn->mn", ket_whole, folded, preferred_element_type=jnp.float32),
        "det",
        scatter_dimension=0,
        tiled=True,
    )


def solution(mesh):
    placed = (P("det", "row", None), P("det"), P("det", None, None))
    return jax.shard_map(
        on_device, mesh=mesh, in_specs=placed, out_specs=P("det", "row"), check_vma=False
    )
```

profile of v0, /device:TPU:0, one launch (start us, length us, event | category | flops | bytes accessed | tf_op | source)
XLA Modules:
  0.0 117.4 jit_solution(16775029854525567413)
XLA Ops:
  6.5 0.0 reduce-scatter.2.cloned.1.call-start
  6.5 0.5 collective-permute-start
  7.0 2.6 %collective-permute-start.1 = (bf16[1,512,200]{1,2,0:T(8,128)(2,1)}, bf16[1,512,200]{1,2,0:T(8,128)(2,1)S(1)}, u32[]{:S(2)}, u32[]{:S(2)}) collective-permute-start(bf16[1,512,200]{1,2,0:T(8,128)(2,1)} %param.3), channel_id=1, source_target_pairs={{28,0},{0,4},{4,8},{8,12},{12,16},{16,20},{20,24},{24,28},{29,1},{... | collective-permute-start | bytes 614408 | tf_op jit(solution)/shard_map/ppermute | solution.py:12
  10.3 20.4 %all_gather.7 = bf16[1,2048,200]{1,2,0:T(8,128)(2,1)S(1)} all-gather(bf16[1,512,200]{1,2,0:T(8,128)(2,1)} %param.3), channel_id=1, replica_groups=mesh['det'=8,'row'=4] {'row'}, dimensions={1}, use_global_device_ids=true | all-gather | bytes 1024000 | tf_op jit(solution)/shard_map/all_gather | solution.py:30
  30.7 0.7 convert_element_type.44
  31.3 0.6 fusion.17
  31.9 0.4 fusion.4
  32.4 0.4 convolution_add_fusion.4
  33.3 0.6 fusion.7
  33.9 1.1 fusion.15
  35.0 0.0 collective-permute-done
  36.3 0.0 collective-permute-done.1
  36.3 18.2 %all_gather.8 = bf16[1,2048,200]{1,2,0:T(8,128)(2,1)S(1)} all-gather(bf16[1,512,200]{1,2,0:T(8,128)(2,1)S(1)} %collective-permute-done.1), channel_id=1, replica_groups=mesh['det'=8,'row'=4] {'row'}, dimensions={1}, use_global_device_ids=true | all-gather | bytes 1024000 | tf_op jit(solution)/shard_map/all_gather | solution.py:38
  54.5 0.4 fusion.6
  55.0 0.4 convolution_add_fusion.3
  55.3 0.6 fusion.8
  55.9 2.9 %convolution_bitcast_fusion = f32[2048,512]{0,1:T(8,128)} fusion(f32[200,512]{1,0:T(8,128)S(1)} %fusion.15, bf16[200,200]{1,0:T(8,128)(2,1)S(1)} %fusion.8, bf16[1,2048,200]{1,2,0:T(8,128)(2,1)S(1)} %all_gather.7, bf16[1,512,200]{1,2,0:T(8,128)(2,1)S(1)} %collective-permute-done.1), kind=kOutput, calls=%fused_computation | convolution fusion | flops 460595200 | bytes 5707904 | tf_op jit(solution)/shard_map/jmb,jbn->mn/dot_general | solution.py:49
  58.8 0.0 reduce-scatter.2.cloned.1.call-update
  58.8 49.7 %reduce-scatter.2.cloned.1.call-done = f32[256,512]{0,1:T(8,128)} async-done(((f32[2048,512]{0,1:T(8,128)}), f32[256,512]{0,1:T(8,128)}) %reduce-scatter.2.cloned.1.call-update) | async-done | bytes 524304 | tf_op jit(solution)/shard_map/reduce_scatter | solution.py:48
  108.6 2.0 %copy.4 = f32[256,512]{1,0:T(8,128)} copy(f32[256,512]{0,1:T(8,128)} %reduce-scatter.2.cloned.1.call-done) | data formatting | bytes 1048576 | tf_op jit(solution)/shard_map/reduce_scatter | solution.py:48
Async XLA Ops:
  6.5 102.0 %reduce-scatter.2.cloned.1.call-start = ((), (), s32[]{:S(2)}) async-start(), calls=%async_computation.1 | async-start | bytes 4718592 | tf_op jit(solution)/shard_map/reduce_scatter | solution.py:48
  6.5 28.5 %collective-permute-start = (bf16[1]{0:T(256)(128)(2,1)}, bf16[1]{0:T(256)(128)(2,1)}, u32[]{:S(2)}, u32[]{:S(2)}) collective-permute-start(bf16[1]{0:T(256)(128)(2,1)} %param.4), channel_id=1, source_target_pairs={{28,0},{0,4},{4,8},{8,12},{12,16},{16,20},{20,24},{24,28},{29,1},{... | collective-permute-start | bytes 14 | tf_op jit(solution)/shard_map/ppermute | solution.py:12
  7.0 29.2 %collective-permute-start.1 = (bf16[1,512,200]{1,2,0:T(8,128)(2,1)}, bf16[1,512,200]{1,2,0:T(8,128)(2,1)S(1)}, u32[]{:S(2)}, u32[]{:S(2)}) collective-permute-start(bf16[1,512,200]{1,2,0:T(8,128)(2,1)} %param.3), channel_id=1, source_target_pairs={{28,0},{0,4},{4,8},{8,12},{12,16},{16,20},{20,24},{24,28},{29,1},{... | collective-permute-start | bytes 614408 | tf_op jit(solution)/shard_map/ppermute | solution.py:12
Sparse Core Ops, SparseCore 0:
  59.0 49.5 reduce-scatter.1
where the time goes:
time: 118 us; the launch traced here: 117 us
  waiting for transfers between devices  49.7 us (42%)
  blocking collectives  38.6 us (33%)
  between operations  15.9 us (13%)
  matrix products  6.78 us (6%)
  starting transfers between devices  3.08 us (3%)
  local copies, waits for them, and re-layouts  2.63 us (2%)
    reduce_scatter x1, waiting for transfers between devices, on_device(): lax.psum_scatter(jnp.einsum('jmb,jbn->mn', ket_whole, folded, preferred_e...  49.7 us
    all_gather x1, blocking collectives, on_device(): ket_whole = lax.all_gather(coefficients, 'row', axis=1, tiled=True)  20.4 us
    all_gather x1, blocking collectives, on_device(): visitor_full = lax.all_gather(visitor[0], 'row', axis=1, tiled=True)  18.2 us
    ppermute x2, starting transfers between devices, shifted(): return lax.ppermute(block, axis, route)  3.08 us
    dot_general x1, matrix products, on_device(): jnp.einsum('jmb,jbn->mn', ket_whole, folded, preferred_element_type=jnp.f...  2.88 us
  transfers between devices with their start and end apart: 3, of which 1 were waited for; matrix products, arithmetic and copies ran while one was open for 3% of the time, Pallas kernels for 0%

commit v1 on v0

v1 whole, which is shorter than its diff:
```python
import functools

import jax
import jax.numpy as jnp
from jax import lax
from jax.experimental import pallas as pl
from jax.experimental.pallas import tpu as pltpu
from jax.sharding import PartitionSpec as P

ORDER = 2
F32 = jnp.float32
BF16 = jnp.bfloat16


def each(count, body):
    if count <= 8:
        for i in range(count):
            body(i)
    else:
        lax.fori_loop(0, count, lambda i, c: (body(i), c)[1], 0)


def inverse_of(correlation):
    size = correlation.shape[0]
    row = lax.broadcasted_iota(jnp.int32, (size, size), 0)
    col = lax.broadcasted_iota(jnp.int32, (size, size), 1)
    identity = jnp.where(row == col, 1.0, 0.0).astype(F32)
    remainder = identity - correlation
    inverse = identity + remainder
    for level in range(ORDER - 1):
        inverse = identity + jnp.dot(
            remainder, inverse, precision=lax.Precision.HIGHEST, preferred_element_type=F32
        )
    return inverse


def gram(a, b):
    return lax.dot_general(a, b, (((0,), (0,)), ((), ())), preferred_element_type=F32)


def against(a, b):
    return lax.dot_general(a, b, (((1,), (1,)), ((), ())), preferred_element_type=F32)


def kernel(
    n, ring, c_ref, amp_ref, mask_ref, out_ref,
    cw, vis, vamp, pw, s0, s1, pieces, folded,
    local_sem, cw_send, cw_recv, pw_send, pw_recv, vis_send, vis_recv,
    piece_send, piece_recv, chip_send, pair_send, folded_recv,
):
    det = lax.axis_index("det")
    row = lax.axis_index("row")
    rows = out_ref.shape[0]
    per_block = n // ring
    chips = n // 2
    chip, core = det // 2, lax.rem(det, 2)
    partner = chip * 2 + (1 - core)
    has_right, has_left = row < ring - 1, row > 0

    def remote(src, dst, send, recv, **where):
        return pltpu.make_async_remote_copy(
            src_ref=src, dst_ref=dst, send_sem=send, recv_sem=recv,
            device_id=where, device_id_type=pl.DeviceIdType.MESH,
        )

    keep = pltpu.make_async_copy(c_ref, cw.at[row], local_sem)
    keep.start()

    barrier = pltpu.get_barrier_semaphore()

    def greet(i):
        peer = lax.rem(det + 1 + i, n)
        pl.semaphore_signal(barrier, inc=1, device_id={"det": peer}, device_id_type=pl.DeviceIdType.MESH)

    each(n - 1, greet)

    @pl.when(has_right)
    def _():
        pl.semaphore_signal(barrier, inc=1, device_id={"row": row + 1}, device_id_type=pl.DeviceIdType.MESH)

    @pl.when(has_left)
    def _():
        pl.semaphore_signal(barrier, inc=1, device_id={"row": row - 1}, device_id_type=pl.DeviceIdType.MESH)

    pl.semaphore_wait(barrier, n - 1 + has_right.astype(jnp.int32) + has_left.astype(jnp.int32))

    def along(buf, sends, recvs, block, side):
        step = 1 if side == 0 else -1
        return remote(
            buf.at[block], buf.at[block], sends.at[block, side], recvs.at[block], row=row + step
        )

    def pass_on(buf, sends, recvs, block, side, wait=False):
        @pl.when(has_right if side == 0 else has_left)
        def _():
            copy = along(buf, sends, recvs, block, side)
            if wait:
                copy.wait_send()
            else:
                copy.start()

    def piece(block, k):
        target = block * per_block + k
        return target, remote(
            cw.at[block, pl.ds(k * rows, rows)], pieces.at[det],
            piece_send.at[block, k], piece_recv.at[det], det=target,
        )

    def hand_out(block, wait=False):
        def one(k):
            target, copy = piece(block, k)

            @pl.when(target != det)
            def _():
                if wait:
                    copy.wait_send()
                else:
                    copy.start()

        each(per_block, one)

    following = lax.rem(det + 1, n)
    visit = remote(c_ref, vis, vis_send.at[0], vis_recv.at[0], det=following)
    visit_amp = remote(amp_ref, vamp, vis_send.at[1], vis_recv.at[1], det=following)
    keep.wait()
    for side in (0, 1):
        pass_on(cw, cw_send, cw_recv, row, side)
    visit.start()
    visit_amp.start()
    s0[...] = gram(c_ref[...], c_ref[...])
    visit.wait_recv()
    hand_out(row)
    s1[...] = gram(vis[...], c_ref[...])
    pw[row] = s1[...]
    for side in (0, 1):
        pass_on(pw, pw_send, pw_recv, row, side)

    for distance in range(1, ring):
        for side in (0, 1):
            block = row - distance if side == 0 else row + distance

            @pl.when((block >= 0) & (block < ring))
            def _():
                along(cw, cw_send, cw_recv, block, side).wait_recv()
                pass_on(cw, cw_send, cw_recv, block, side)
                hand_out(block)
                s0[...] += gram(cw[block], cw[block])

        for side in (0, 1):
            block = row - distance if side == 0 else row + distance

            @pl.when((block >= 0) & (block < ring))
            def _():
                along(pw, pw_send, pw_recv, block, side).wait_recv()
                pass_on(pw, pw_send, pw_recv, block, side)
                s1[...] += pw[block]

    visit_amp.wait_recv()
    amp = amp_ref[0:1, 0:1]
    weight = amp * amp * mask_ref[0, 0:1, 0:1]
    scaled = (weight * inverse_of(s0[...])).astype(BF16)
    total = against(scaled, c_ref[...])
    weight = vamp[0:1, 0:1] * amp * mask_ref[1, 0:1, 0:1]
    scaled = (weight * inverse_of(s1[...])).astype(BF16)
    folded[det] = (total + against(scaled, vis[...])).astype(BF16)

    def to_chip(i):
        target = lax.rem(chip + 1 + i, chips) * 2 + core
        return remote(folded.at[det], folded.at[det], chip_send.at[i], folded_recv.at[det], det=target)

    def to_pair(source):
        return remote(
            folded.at[source], folded.at[source], pair_send.at[source], folded_recv.at[source], det=partner
        )

    each(chips - 1, lambda i: to_chip(i).start())
    to_pair(det).start()

    def landed(source):
        to_pair(source).wait_recv()

    def add(source):
        remote(
            cw.at[0, pl.ds(0, rows)], pieces.at[source], piece_send.at[0, 0], piece_recv.at[source], det=partner
        ).wait_recv()
        out_ref[...] += jnp.dot(pieces[source], folded[source], preferred_element_type=F32)

    own_block, own_part = det // per_block, lax.rem(det, per_block)
    mine = cw[own_block, pl.ds(pl.multiple_of(own_part * rows, rows), rows)]
    out_ref[...] = jnp.dot(mine, folded[det], preferred_element_type=F32)
    landed(partner)
    add(partner)

    def relay(i):
        other = lax.rem(chip + chips - 1 - i, chips) * 2
        landed(other + core)
        to_pair(other + core).start()
        add(other + core)

    def relayed(i):
        other = lax.rem(chip + chips - 1 - i, chips) * 2
        landed(other + 1 - core)
        add(other + 1 - core)

    each(chips - 1, relay)
    each(chips - 1, relayed)

    visit.wait_send()
    visit_amp.wait_send()
    for side in (0, 1):
        pass_on(cw, cw_send, cw_recv, row, side, wait=True)
        pass_on(pw, pw_send, pw_recv, row, side, wait=True)
    hand_out(row, wait=True)
    for distance in range(1, ring):
        for side in (0, 1):
            block = row - distance if side == 0 else row + distance

            @pl.when((block >= 0) & (block < ring))
            def _():
                pass_on(cw, cw_send, cw_recv, block, side, wait=True)
                pass_on(pw, pw_send, pw_recv, block, side, wait=True)
                hand_out(block, wait=True)

    each(chips - 1, lambda i: to_chip(i).wait_send())
    to_pair(det).wait_send()
    each(chips - 1, lambda i: to_pair(lax.rem(chip + chips - 1 - i, chips) * 2 + core).wait_send())


def on_device(coefficients, amplitudes, plan):
    n, ring = lax.axis_size("det"), lax.axis_size("row")
    block = coefficients[0]
    size, orbitals = block.shape
    steps = plan.shape[1]
    if coefficients.shape[0] != 1 or steps != 2:
        raise ValueError("unsupported sizes")
    rows = size * ring // n
    amp = jnp.broadcast_to(amplitudes.astype(F32)[:, None], (8, 128))
    masks = jnp.broadcast_to(plan.astype(F32).reshape(steps, 1, 1), (steps, 8, 128))
    dma = pltpu.SemaphoreType.DMA
    return pl.pallas_call(
        functools.partial(kernel, n, ring),
        out_shape=jax.ShapeDtypeStruct((rows, size), F32),
        in_specs=[pl.BlockSpec(memory_space=pltpu.VMEM)] * 3,
        out_specs=pl.BlockSpec(memory_space=pltpu.VMEM),
        scratch_shapes=[
            pltpu.VMEM((ring, size, orbitals), BF16),
            pltpu.VMEM((size, orbitals), BF16),
            pltpu.VMEM((8, 128), F32),
            pltpu.VMEM((ring, orbitals, orbitals), F32),
            pltpu.VMEM((orbitals, orbitals), F32),
            pltpu.VMEM((orbitals, orbitals), F32),
            pltpu.VMEM((n, rows, orbitals), BF16),
            pltpu.VMEM((n, orbitals, size), BF16),
            dma, dma((ring, 2)), dma((ring,)), dma((ring, 2)), dma((ring,)), dma((2,)), dma((2,)),
            dma((ring, n // ring)), dma((n,)), dma((n // 2,)), dma((n,)), dma((n,)),
        ],
        compiler_params=pltpu.CompilerParams(
            collective_id=0, has_side_effects=True, vmem_limit_bytes=60 * 1024 * 1024
        ),
    )(block, amp, masks)


def solution(mesh):
    placed = (P("det", "row", None), P("det"), P("det", None, None))
    return jax.shard_map(
        on_device, mesh=mesh, in_specs=placed, out_specs=P("det", "row"), check_vma=False
    )
```

time: 118 us -> 61.5 us (0.52)
  the two profiles are of different devices: /device:TPU:0 before, /device:TPU:7 now
where the time goes in v1:
time: 61.5 us; the launch traced here: 61.3 us
  Pallas kernels  55.1 us (90%)
  local copies, waits for them, and re-layouts  5.54 us (9%)
  between operations  0.68 us (1%)
    pallas_call x1, Pallas kernels, on_device(): pl.pallas_call(functools.partial(kernel, n, ring), out_shape=jax.ShapeDty...  55.1 us
    unnamed x4, local copies, waits for them, and re-layouts  4.29 us

profile of v1, /device:TPU:7, one launch (start us, length us, event | category | flops | bytes accessed | tf_op | source)
XLA Modules:
  0.0 61.3 jit_solution(7919777516214697026)
XLA Ops:
  0.7 0.0 copy-start
  0.7 0.6 %copy-done = s32[1,2,1]{1,2,0:T(1,128)S(1)} copy-done((s32[1,2,1]{1,2,0:T(1,128)S(1)}, s32[1,2,1]{1,2,0:T(1,128)}, u32[]{:S(2)}) %copy-start) | copy-done | bytes 32
  1.3 0.6 broadcast_in_dim.20.amp_ref
  1.9 0.7 %broadcast_in_dim.22.mask_ref = f32[2,8,128]{2,1,0:T(8,128)} broadcast(f32[2]{0:T(128)S(1)} %convert_bitcast_fusion), dimensions={0} | broadcast | bytes 8200 | tf_op jit(solution)/shard_map/broadcast_in_dim | solution.py:238
  2.6 1.8 %copy.4 = bf16[1,512,200]{2,1,0:T(8,128)(2,1)} copy(bf16[1,512,200]{1,2,0:T(8,128)(2,1)} %param.3) | data formatting | bytes 409600 | tf_op args[0]
  4.3 55.1 %shard_map.37 = f32[256,512]{1,0:T(8,128)} custom-call(bf16[512,200]{1,0:T(8,128)(2,1)} %bitcast.6, f32[8,128]{1,0:T(8,128)} %broadcast_in_dim.20.amp_ref, f32[2,8,128]{2,1,0:T(8,128)} %broadcast_in_dim.22.mask_ref), custom_call_target="tpu_custom_call" | custom-call | tf_op jit(solution)/shard_map/pallas_call | solution.py:240
  59.4 1.9 %copy.7 = f32[256,512]{1,0:T(8,128)} copy(f32[256,512]{1,0:T(8,128)} %shard_map.37) | data formatting | bytes 1048576
  (1 shorter events, 0.0 us)
Async XLA Ops:
  0.7 0.7 %copy-start = (s32[1,2,1]{1,2,0:T(1,128)S(1)}, s32[1,2,1]{1,2,0:T(1,128)}, u32[]{:S(2)}) copy-start(s32[1,2,1]{1,2,0:T(1,128)} %param.5) | copy-start | bytes 28

commit v2 on v1

v2 whole, which is shorter than its diff:
```python
import functools

import jax
import jax.numpy as jnp
from jax import lax
from jax.experimental import pallas as pl
from jax.experimental.pallas import tpu as pltpu
from jax.sharding import PartitionSpec as P

ORDER = 2
F32 = jnp.float32
BF16 = jnp.bfloat16


def each(count, body):
    if count <= 8:
        for i in range(count):
            body(i)
    else:
        lax.fori_loop(0, count, lambda i, c: (body(i), c)[1], 0)


def inverse_of(correlation):
    size = correlation.shape[0]
    row = lax.broadcasted_iota(jnp.int32, (size, size), 0)
    col = lax.broadcasted_iota(jnp.int32, (size, size), 1)
    identity = jnp.where(row == col, 1.0, 0.0).astype(F32)
    remainder = identity - correlation
    inverse = identity + remainder
    for level in range(ORDER - 1):
        inverse = identity + jnp.dot(
            remainder, inverse, precision=lax.Precision.HIGHEST, preferred_element_type=F32
        )
    return inverse


def gram(a, b):
    return lax.dot_general(a, b, (((0,), (0,)), ((), ())), preferred_element_type=F32)


def against(a, b):
    return lax.dot_general(a, b, (((1,), (1,)), ((), ())), preferred_element_type=F32)


def parts_of(size, count):
    step = -(-size // (8 * count)) * 8
    return [(start, min(step, size - start)) for start in range(0, size, step)]


def kernel(
    n, ring, c_ref, amp_ref, plan_ref, out_ref,
    cw, vis, amps, own, sum_in, sum_out, s0, pieces, folded, wide,
    local_sem, cw_send, cw_recv, sum_send, sum_recv, vis_send, vis_recv,
    piece_send, piece_recv, chip_send, pair_send, folded_recv,
):
    det = lax.axis_index("det")
    row = lax.axis_index("row")
    rows = out_ref.shape[0]
    width = pieces.shape[2]
    per_block = n // ring
    chips = n // 2
    chip, core = det // 2, lax.rem(det, 2)
    partner = chip * 2 + (1 - core)
    has_right, has_left = row < ring - 1, row > 0
    toward = (has_right, has_left)
    chunks = parts_of(own.shape[0], 4)

    def remote(src, dst, send, recv, **where):
        return pltpu.make_async_remote_copy(
            src_ref=src, dst_ref=dst, send_sem=send, recv_sem=recv,
            device_id=where, device_id_type=pl.DeviceIdType.MESH,
        )

    keep = pltpu.make_async_copy(c_ref, cw.at[row], local_sem)
    keep.start()

    barrier = pltpu.get_barrier_semaphore()

    def greet(i):
        peer = lax.rem(det + 1 + i, n)
        pl.semaphore_signal(barrier, inc=1, device_id={"det": peer}, device_id_type=pl.DeviceIdType.MESH)

    each(n - 1, greet)

    for side in (0, 1):

        @pl.when(toward[side])
        def _():
            peer = row + 1 - 2 * side
            pl.semaphore_signal(barrier, inc=1, device_id={"row": peer}, device_id_type=pl.DeviceIdType.MESH)

    amps[0] = jnp.broadcast_to(amp_ref[...].astype(F32), amps.shape[1:])
    pl.semaphore_wait(barrier, n - 1 + has_right.astype(jnp.int32) + has_left.astype(jnp.int32))

    def along(block, side):
        return remote(
            cw.at[block], cw.at[block], cw_send.at[block, side], cw_recv.at[block], row=row + 1 - 2 * side
        )

    def pass_on(block, side, wait=False):
        @pl.when(toward[side])
        def _():
            copy = along(block, side)
            if wait:
                copy.wait_send()
            else:
                copy.start()

    def chunk_copy(k, side):
        span = pl.ds(*chunks[k])
        return remote(
            sum_out.at[side, span], sum_in.at[side, span], sum_send.at[side, k], sum_recv.at[side, k],
            row=row + 1 - 2 * side,
        )

    def sums(side, first):
        for k, (start, length) in enumerate(chunks):
            span = pl.ds(start, length)
            if first:
                sum_in[side, span] = jnp.zeros((length, own.shape[1]), F32)
                sum_out[side, span] = own[span]
            else:
                chunk_copy(k, side).wait_recv()
                sum_out[side, span] = own[span] + sum_in[side, span]

            @pl.when(toward[side])
            def _():
                chunk_copy(k, side).start()

    def piece(block, k):
        target = block * per_block + k
        start = pl.multiple_of(k * rows // width * width, width)
        return target, remote(
            cw.at[block, :, pl.ds(start, width)], pieces.at[det],
            piece_send.at[block, k], piece_recv.at[det], det=target,
        )

    def hand_out(block, wait=False):
        def one(k):
            target, copy = piece(block, k)

            @pl.when(target != det)
            def _():
                if wait:
                    copy.wait_send()
                else:
                    copy.start()

        each(per_block, one)

    following = lax.rem(det + 1, n)
    visit = remote(c_ref, vis, vis_send.at[0], vis_recv.at[0], det=following)
    visit_amp = remote(amps.at[0], amps.at[1], vis_send.at[1], vis_recv.at[1], det=following)
    visit.start()
    visit_amp.start()
    keep.wait()
    for side in (0, 1):
        pass_on(row, side)
    s0[...] = against(c_ref[...], c_ref[...])
    visit.wait_recv()
    own[...] = against(vis[...], c_ref[...])

    @pl.when(row == 0)
    def _():
        sums(0, True)

    @pl.when(row == ring - 1)
    def _():
        sums(1, True)

    hand_out(row)

    def arrive(distance):
        for side in (0, 1):
            block = row - distance if side == 0 else row + distance

            @pl.when((block >= 0) & (block < ring))
            def _():
                along(block, side).wait_recv()
                pass_on(block, side)
                hand_out(block)
                s0[...] += against(cw[block], cw[block])

    def gather_sums(distance):
        @pl.when(row == distance)
        def _():
            sums(0, False)

        @pl.when(row == ring - 1 - distance)
        def _():
            sums(1, False)

    for distance in range(1, ring - 1):
        arrive(distance)
        gather_sums(distance)
    arrive(ring - 1)
    visit_amp.wait_recv()
    amp = amps[0, 0:1, 0:1]
    masks = plan_ref[...].astype(F32)
    weight = amp * amp * masks[0:1, 0:1]
    scaled = (weight * inverse_of(s0[...])).astype(BF16)
    total = jnp.dot(scaled, c_ref[...], preferred_element_type=F32)
    gather_sums(ring - 1)
    weight = amps[1, 0:1, 0:1] * amp * masks[1:2, 0:1]
    correlation = own[...] + sum_in[0] + sum_in[1]
    scaled = (weight * inverse_of(correlation)).astype(BF16)
    total = total + jnp.dot(scaled, vis[...], preferred_element_type=F32)
    folded[det] = total.astype(BF16)

    def to_chip(i):
        target = lax.rem(chip + 1 + i, chips) * 2 + core
        return remote(folded.at[det], folded.at[det], chip_send.at[i], folded_recv.at[det], det=target)

    def to_pair(source):
        return remote(
            folded.at[source], folded.at[source], pair_send.at[source], folded_recv.at[source], det=partner
        )

    each(chips - 1, lambda i: to_chip(i).start())
    to_pair(det).start()

    def landed(source):
        to_pair(source).wait_recv()

    sink = out_ref if width == rows else wide

    def add(source):
        remote(
            cw.at[0, :, pl.ds(0, width)], pieces.at[source], piece_send.at[0, 0], piece_recv.at[source],
            det=partner,
        ).wait_recv()
        sink[...] += gram(pieces[source], folded[source])

    own_start = lax.rem(det, per_block) * rows // width * width
    mine = cw[det // per_block, :, pl.ds(pl.multiple_of(own_start, width), width)]
    sink[...] = gram(mine, folded[det])
    landed(partner)
    add(partner)

    def relay(i):
        other = lax.rem(chip + chips - 1 - i, chips) * 2
        landed(other + core)
        to_pair(other + core).start()
        add(other + core)

    def relayed(i):
        other = lax.rem(chip + chips - 1 - i, chips) * 2
        landed(other + 1 - core)
        add(other + 1 - core)

    each(chips - 1, relay)
    each(chips - 1, relayed)
    if width != rows:
        out_ref[...] = wide[pl.ds(pl.multiple_of(lax.rem(det * rows, width), rows), rows)]

    visit.wait_send()
    visit_amp.wait_send()
    for side in (0, 1):
        pass_on(row, side, wait=True)

        @pl.when(toward[side])
        def _():
            for k in range(len(chunks)):
                chunk_copy(k, side).wait_send()

    hand_out(row, wait=True)
    for distance in range(1, ring):
        for side in (0, 1):
            block = row - distance if side == 0 else row + distance

            @pl.when((block >= 0) & (block < ring))
            def _():
                pass_on(block, side, wait=True)
                hand_out(block, wait=True)

    each(chips - 1, lambda i: to_chip(i).wait_send())
    to_pair(det).wait_send()
    each(chips - 1, lambda i: to_pair(lax.rem(chip + chips - 1 - i, chips) * 2 + core).wait_send())


def on_device(coefficients, amplitudes, plan):
    n, ring = lax.axis_size("det"), lax.axis_size("row")
    if coefficients.shape[0] != 1 or plan.shape[1] != 2:
        raise ValueError("unsupported sizes")
    block = jnp.swapaxes(coefficients, 1, 2)[0]
    orbitals, size = block.shape
    rows = size * ring // n
    width = max(rows, 128)
    dma = pltpu.SemaphoreType.DMA
    return pl.pallas_call(
        functools.partial(kernel, n, ring),
        out_shape=jax.ShapeDtypeStruct((rows, size), F32),
        in_specs=[pl.BlockSpec(memory_space=pltpu.VMEM)] * 3,
        out_specs=pl.BlockSpec(memory_space=pltpu.VMEM),
        scratch_shapes=[
            pltpu.VMEM((ring, orbitals, size), BF16),
            pltpu.VMEM((orbitals, size), BF16),
            pltpu.VMEM((2, 8, 128), F32),
            pltpu.VMEM((orbitals, orbitals), F32),
            pltpu.VMEM((2, orbitals, orbitals), F32),
            pltpu.VMEM((2, orbitals, orbitals), F32),
            pltpu.VMEM((orbitals, orbitals), F32),
            pltpu.VMEM((n, orbitals, width), BF16),
            pltpu.VMEM((n, orbitals, size), BF16),
            pltpu.VMEM((width, size) if width != rows else (8, 128), F32),
            dma, dma((ring, 2)), dma((ring,)), dma((2, 4)), dma((2, 4)), dma((2,)), dma((2,)),
            dma((ring, n // ring)), dma((n,)), dma((n // 2,)), dma((n,)), dma((n,)),
        ],
        compiler_params=pltpu.CompilerParams(
            collective_id=0, has_side_effects=True, vmem_limit_bytes=60 * 1024 * 1024
        ),
    )(block, amplitudes.reshape(1, 1), plan.reshape(2, 1))


def solution(mesh):
    placed = (P("det", "row", None), P("det"), P("det", None, None))
    return jax.shard_map(
        on_device, mesh=mesh, in_specs=placed, out_specs=P("det", "row"), check_vma=False
    )
```

time: 61.5 us -> 45.4 us (0.74)
  Pallas kernels: 55.1 us -> 41.4 us
  local copies, waits for them, and re-layouts: 5.54 us -> 3.16 us
    pallas_call x1, Pallas kernels: 55.1 us -> 41.4 us  [on_device(): pl.pallas_call(functools.partial(kernel, n, ring), out_shape=jax.ShapeDty...]
    unnamed x4 -> x3, local copies, waits for them, and re-layouts: 4.29 us -> 2.52 us
    broadcast_in_dim x2 -> x0, local copies, waits for them, and re-layouts: 1.26 us -> none  [the longest x1 0.66 us: on_device(): jnp.broadcast_to(plan.astype(F32).reshape(steps, 1, 1), (steps, 8, 128))]
    reshape x0 -> x1, local copies, waits for them, and re-layouts: none -> 0.65 us  [on_device(): plan.reshape(2, 1)]
where the time goes in v2:
time: 45.4 us; the launch traced here: 45.3 us
  Pallas kernels  41.4 us (91%)
  local copies, waits for them, and re-layouts  3.16 us (7%)
  between operations  0.68 us (1%)
    pallas_call x1, Pallas kernels, on_device(): pl.pallas_call(functools.partial(kernel, n, ring), out_shape=jax.ShapeDty...  41.4 us
    unnamed x3, local copies, waits for them, and re-layouts  2.52 us

profile of v2, /device:TPU:7, one launch (start us, length us, event | category | flops | bytes accessed | tf_op | source)
XLA Modules:
  0.0 45.3 jit_solution(6406103347301552367)
XLA Ops:
  0.7 0.0 copy-start
  0.7 0.6 %copy-done = s32[1,2,1]{1,2,0:T(1,128)S(1)} copy-done((s32[1,2,1]{1,2,0:T(1,128)S(1)}, s32[1,2,1]{1,2,0:T(1,128)}, u32[]{:S(2)}) %copy-start) | copy-done | bytes 32
  1.3 0.6 %copy.4.plan_ref = s32[2,1]{1,0:T(2,128)} copy(s32[2,1]{0,1:T(1,128)S(1)} %bitcast.7) | data formatting | bytes 16 | tf_op jit(solution)/shard_map/reshape | solution.py:312
  2.0 41.4 %shard_map.37 = f32[256,512]{1,0:T(8,128)} custom-call(bf16[200,512]{1,0:T(8,128)(2,1)} %bitcast.6, bf16[1,1]{1,0:T(2,128)(2,1)} %bitcast.5.amp_ref, s32[2,1]{1,0:T(2,128)} %copy.4.plan_ref), custom_call_target="tpu_custom_call" | custom-call | tf_op jit(solution)/shard_map/pallas_call | solution.py:290
  43.4 1.9 %copy.7 = f32[256,512]{1,0:T(8,128)} copy(f32[256,512]{1,0:T(8,128)} %shard_map.37) | data formatting | bytes 1048576
Async XLA Ops:
  0.7 0.7 %copy-start = (s32[1,2,1]{1,2,0:T(1,128)S(1)}, s32[1,2,1]{1,2,0:T(1,128)}, u32[]{:S(2)}) copy-start(s32[1,2,1]{1,2,0:T(1,128)} %param.5) | copy-start | bytes 28

commit v3 on v2

--- a/solution.py
+++ b/solution.py
@@ -49,7 +49,7 @@
 
 def kernel(
     n, ring, c_ref, amp_ref, plan_ref, out_ref,
-    cw, vis, amps, own, sum_in, sum_out, s0, pieces, folded, wide,
+    cw, vis, amps, own, sum_in, sum_out, pieces, folded, wide,
     local_sem, cw_send, cw_recv, sum_send, sum_recv, vis_send, vis_recv,
     piece_send, piece_recv, chip_send, pair_send, folded_recv,
 ):
@@ -63,7 +63,7 @@
     partner = chip * 2 + (1 - core)
     has_right, has_left = row < ring - 1, row > 0
     toward = (has_right, has_left)
-    chunks = parts_of(own.shape[0], 4)
+    chunks = parts_of(own.shape[1], 4)
 
     def remote(src, dst, send, recv, **where):
         return pltpu.make_async_remote_copy(
@@ -92,40 +92,50 @@
     amps[0] = jnp.broadcast_to(amp_ref[...].astype(F32), amps.shape[1:])
     pl.semaphore_wait(barrier, n - 1 + has_right.astype(jnp.int32) + has_left.astype(jnp.int32))
 
-    def along(block, side):
+    def along(block, side, half):
+        span = cw.at[block, :, pl.ds(half * (cw.shape[2] // 2), cw.shape[2] // 2)]
         return remote(
-            cw.at[block], cw.at[block], cw_send.at[block, side], cw_recv.at[block], row=row + 1 - 2 * side
-        )
-
-    def pass_on(block, side, wait=False):
+            span, span, cw_send.at[block, side, half], cw_recv.at[block, half], row=row + 1 - 2 * side
+        )
+
+    def pass_on(block, side, half, wait=False):
         @pl.when(toward[side])
         def _():
-            copy = along(block, side)
+            copy = along(block, side, half)
             if wait:
                 copy.wait_send()
             else:
                 copy.start()
 
-    def chunk_copy(k, side):
+    def chunk_copy(which, k, side):
         span = pl.ds(*chunks[k])
         return remote(
-            sum_out.at[side, span], sum_in.at[side, span], sum_send.at[side, k], sum_recv.at[side, k],
-            row=row + 1 - 2 * side,
-        )
-
-    def sums(side, first):
+            sum_out.at[which, side, span], sum_in.at[which, side, span],
+            sum_send.at[which, side, k], sum_recv.at[which, side, k], row=row + 1 - 2 * side,
+        )
+
+    def sums(which, side, first):
         for k, (start, length) in enumerate(chunks):
             span = pl.ds(start, length)
             if first:
-                sum_in[side, span] = jnp.zeros((length, own.shape[1]), F32)
-                sum_out[side, span] = own[span]
+                sum_in[which, side, span] = jnp.zeros((length, own.shape[2]), F32)
+                sum_out[which, side, span] = own[which, span]
             else:
-                chunk_copy(k, side).wait_recv()
-                sum_out[side, span] = own[span] + sum_in[side, span]
+                chunk_copy(which, k, side).wait_recv()
+                sum_out[which, side, span] = own[which, span] + sum_in[which, side, span]
 
             @pl.when(toward[side])
             def _():
-                chunk_copy(k, side).start()
+                chunk_copy(which, k, side).start()
+
+    def open_sums(which):
+        @pl.when(row == 0)
+        def _():
+            sums(which, 0, True)
+
+        @pl.when(row == ring - 1)
+        def _():
+            sums(which, 1, True)
 
     def piece(block, k):
         target = block * per_block + k
@@ -135,9 +145,9 @@
             piece_send.at[block, k], piece_recv.at[det], det=target,
         )
 
-    def hand_out(block, wait=False):
-        def one(k):
-            target, copy = piece(block, k)
+    def hand_out(block, half, wait=False):
+        def one(part):
+            target, copy = piece(block, half * (per_block // 2) + part)
 
             @pl.when(target != det)
             def _():
@@ -146,7 +156,7 @@
                 else:
                     copy.start()
 
-        each(per_block, one)
+        each(per_block // 2, one)
 
     following = lax.rem(det + 1, n)
     visit = remote(c_ref, vis, vis_send.at[0], vis_recv.at[0], det=following)
@@ -154,57 +164,56 @@
     visit.start()
     visit_amp.start()
     keep.wait()
-    for side in (0, 1):
-        pass_on(row, side)
-    s0[...] = against(c_ref[...], c_ref[...])
+    for half in (0, 1):
+        for side in (0, 1):
+            pass_on(row, side, half)
+    own[0] = against(c_ref[...], c_ref[...])
+    open_sums(0)
     visit.wait_recv()
-    own[...] = against(vis[...], c_ref[...])
-
-    @pl.when(row == 0)
-    def _():
-        sums(0, True)
-
-    @pl.when(row == ring - 1)
-    def _():
-        sums(1, True)
-
-    hand_out(row)
+    own[1] = against(vis[...], c_ref[...])
+    open_sums(1)
+    for half in (0, 1):
+        hand_out(row, half)
 
     def arrive(distance):
-        for side in (0, 1):
-            block = row - distance if side == 0 else row + distance
-
-            @pl.when((block >= 0) & (block < ring))
+        for half in (0, 1):
+            for side in (0, 1):
+                block = row - distance if side == 0 else row + distance
+
+                @pl.when((block >= 0) & (block < ring))
+                def _():
+                    along(block, side, half).wait_recv()
+                    pass_on(block, side, half)
+                    hand_out(block, half)
+
+    def gather_sums(distance):
+        for which in (0, 1):
+
+            @pl.when(row == distance)
             def _():
-                along(block, side).wait_recv()
-                pass_on(block, side)
-                hand_out(block)
-                s0[...] += against(cw[block], cw[block])
-
-    def gather_sums(distance):
-        @pl.when(row == distance)
-        def _():
-            sums(0, False)
-
-        @pl.when(row == ring - 1 - distance)
-        def _():
-            sums(1, False)
-
-    for distance in range(1, ring - 1):
+                sums(which, 0, False)
+
+            @pl.when(row == ring - 1 - distance)
+            def _():
+                sums(which, 1, False)
+
+    arrive(1)
+    gather_sums(1)
+    for distance in range(2, ring - 1):
+        gather_sums(distance)
         arrive(distance)
-        gather_sums(distance)
-    arrive(ring - 1)
+    gather_sums(ring - 1)
     visit_amp.wait_recv()
     amp = amps[0, 0:1, 0:1]
     masks = plan_ref[...].astype(F32)
-    weight = amp * amp * masks[0:1, 0:1]
-    scaled = (weight * inverse_of(s0[...])).astype(BF16)
-    total = jnp.dot(scaled, c_ref[...], preferred_element_type=F32)
-    gather_sums(ring - 1)
-    weight = amps[1, 0:1, 0:1] * amp * masks[1:2, 0:1]
-    correlation = own[...] + sum_in[0] + sum_in[1]
-    scaled = (weight * inverse_of(correlation)).astype(BF16)
-    total = total + jnp.dot(scaled, vis[...], preferred_element_type=F32)
+
+    def scaled(which):
+        weight = amps[which, 0:1, 0:1] * amp * masks[which:which + 1, 0:1]
+        correlation = own[which] + sum_in[which, 0] + sum_in[which, 1]
+        return (weight * inverse_of(correlation)).astype(BF16)
+
+    total = jnp.dot(scaled(0), c_ref[...], preferred_element_type=F32)
+    total = total + jnp.dot(scaled(1), vis[...], preferred_element_type=F32)
     folded[det] = total.astype(BF16)
 
     def to_chip(i):
@@ -218,6 +227,7 @@
 
     each(chips - 1, lambda i: to_chip(i).start())
     to_pair(det).start()
+    arrive(ring - 1)
 
     def landed(source):
         to_pair(source).wait_recv()
@@ -256,22 +266,25 @@
     visit.wait_send()
     visit_amp.wait_send()
     for side in (0, 1):
-        pass_on(row, side, wait=True)
 
         @pl.when(toward[side])
         def _():
-            for k in range(len(chunks)):
-                chunk_copy(k, side).wait_send()
-
-    hand_out(row, wait=True)
-    for distance in range(1, ring):
+            for which in (0, 1):
+                for k in range(len(chunks)):
+                    chunk_copy(which, k, side).wait_send()
+
+    for half in (0, 1):
         for side in (0, 1):
-            block = row - distance if side == 0 else row + distance
-
-            @pl.when((block >= 0) & (block < ring))
-            def _():
-                pass_on(block, side, wait=True)
-                hand_out(block, wait=True)
+            pass_on(row, side, half, wait=True)
+        hand_out(row, half, wait=True)
+        for distance in range(1, ring):
+            for side in (0, 1):
+                block = row - distance if side == 0 else row + distance
+
+                @pl.when((block >= 0) & (block < ring))
+                def _():
+                    pass_on(block, side, half, wait=True)
+                    hand_out(block, half, wait=True)
 
     each(chips - 1, lambda i: to_chip(i).wait_send())
     to_pair(det).wait_send()
@@ -296,14 +309,13 @@
             pltpu.VMEM((ring, orbitals, size), BF16),
             pltpu.VMEM((orbitals, size), BF16),
             pltpu.VMEM((2, 8, 128), F32),
-            pltpu.VMEM((orbitals, orbitals), F32),
             pltpu.VMEM((2, orbitals, orbitals), F32),
-            pltpu.VMEM((2, orbitals, orbitals), F32),
-            pltpu.VMEM((orbitals, orbitals), F32),
+            pltpu.VMEM((2, 2, orbitals, orbitals), F32),
+            pltpu.VMEM((2, 2, orbitals, orbitals), F32),
             pltpu.VMEM((n, orbitals, width), BF16),
             pltpu.VMEM((n, orbitals, size), BF16),
             pltpu.VMEM((width, size) if width != rows else (8, 128), F32),
-            dma, dma((ring, 2)), dma((ring,)), dma((2, 4)), dma((2, 4)), dma((2,)), dma((2,)),
+            dma, dma((ring, 2, 2)), dma((ring, 2)), dma((2, 2, 4)), dma((2, 2, 4)), dma((2,)), dma((2,)),
             dma((ring, n // ring)), dma((n,)), dma((n // 2,)), dma((n,)), dma((n,)),
         ],
         compiler_params=pltpu.CompilerParams(

time: 45.4 us -> 54 us (1.19); the launches traced: 45.3 us -> 53.1 us
  Pallas kernels: 41.4 us -> 49.2 us
    pallas_call x1, Pallas kernels: 41.4 us -> 49.2 us  [on_device(): pl.pallas_call(functools.partial(kernel, n, ring), out_shape=jax.ShapeDty...]
where the time goes in v3:
time: 54 us; the launch traced here: 53.1 us
  Pallas kernels  49.2 us (91%)
  local copies, waits for them, and re-layouts  3.16 us (6%)
  between operations  0.68 us (1%)
    pallas_call x1, Pallas kernels, on_device(): pl.pallas_call(functools.partial(kernel, n, ring), out_shape=jax.ShapeDty...  49.2 us
    unnamed x3, local copies, waits for them, and re-layouts  2.52 us

profile of v3, /device:TPU:7, one launch (start us, length us, event | category | flops | bytes accessed | tf_op | source)
XLA Modules:
  0.0 53.1 jit_solution(4377283915037255488)
XLA Ops:
  0.7 0.0 copy-start
  0.7 0.6 %copy-done = s32[1,2,1]{1,2,0:T(1,128)S(1)} copy-done((s32[1,2,1]{1,2,0:T(1,128)S(1)}, s32[1,2,1]{1,2,0:T(1,128)}, u32[]{:S(2)}) %copy-start) | copy-done | bytes 32
  1.3 0.6 %copy.4.plan_ref = s32[2,1]{1,0:T(2,128)} copy(s32[2,1]{0,1:T(1,128)S(1)} %bitcast.7) | data formatting | bytes 16 | tf_op jit(solution)/shard_map/reshape | solution.py:324
  2.0 49.2 %shard_map.37 = f32[256,512]{1,0:T(8,128)} custom-call(bf16[200,512]{1,0:T(8,128)(2,1)} %bitcast.6, bf16[1,1]{1,0:T(2,128)(2,1)} %bitcast.5.amp_ref, s32[2,1]{1,0:T(2,128)} %copy.4.plan_ref), custom_call_target="tpu_custom_call" | custom-call | tf_op jit(solution)/shard_map/pallas_call | solution.py:303
  51.2 1.9 %copy.7 = f32[256,512]{1,0:T(8,128)} copy(f32[256,512]{1,0:T(8,128)} %shard_map.37) | data formatting | bytes 1048576
Async XLA Ops:
  0.7 0.7 %copy-start = (s32[1,2,1]{1,2,0:T(1,128)S(1)}, s32[1,2,1]{1,2,0:T(1,128)}, u32[]{:S(2)}) copy-start(s32[1,2,1]{1,2,0:T(1,128)} %param.5) | copy-start | bytes 28

commit v4 on v2

--- a/solution.py
+++ b/solution.py
@@ -92,15 +92,18 @@
     amps[0] = jnp.broadcast_to(amp_ref[...].astype(F32), amps.shape[1:])
     pl.semaphore_wait(barrier, n - 1 + has_right.astype(jnp.int32) + has_left.astype(jnp.int32))
 
-    def along(block, side):
+    halves = parts_of(own.shape[0], 2)
+
+    def along(block, side, half):
+        span = cw.at[block, pl.ds(*halves[half])]
         return remote(
-            cw.at[block], cw.at[block], cw_send.at[block, side], cw_recv.at[block], row=row + 1 - 2 * side
-        )
-
-    def pass_on(block, side, wait=False):
+            span, span, cw_send.at[block, side, half], cw_recv.at[block, half], row=row + 1 - 2 * side
+        )
+
+    def pass_on(block, side, half, wait=False):
         @pl.when(toward[side])
         def _():
-            copy = along(block, side)
+            copy = along(block, side, half)
             if wait:
                 copy.wait_send()
             else:
@@ -154,8 +157,9 @@
     visit.start()
     visit_amp.start()
     keep.wait()
-    for side in (0, 1):
-        pass_on(row, side)
+    for half in (0, 1):
+        for side in (0, 1):
+            pass_on(row, side, half)
     s0[...] = against(c_ref[...], c_ref[...])
     visit.wait_recv()
     own[...] = against(vis[...], c_ref[...])
@@ -176,8 +180,16 @@
 
             @pl.when((block >= 0) & (block < ring))
             def _():
-                along(block, side).wait_recv()
-                pass_on(block, side)
+                along(block, side, 0).wait_recv()
+                pass_on(block, side, 0)
+
+        for side in (0, 1):
+            block = row - distance if side == 0 else row + distance
+
+            @pl.when((block >= 0) & (block < ring))
+            def _():
+                along(block, side, 1).wait_recv()
+                pass_on(block, side, 1)
                 hand_out(block)
                 s0[...] += against(cw[block], cw[block])
 
@@ -256,7 +268,8 @@
     visit.wait_send()
     visit_amp.wait_send()
     for side in (0, 1):
-        pass_on(row, side, wait=True)
+        for half in (0, 1):
+            pass_on(row, side, half, wait=True)
 
         @pl.when(toward[side])
         def _():
@@ -270,7 +283,8 @@
 
             @pl.when((block >= 0) & (block < ring))
             def _():
-                pass_on(block, side, wait=True)
+                for half in (0, 1):
+                    pass_on(block, side, half, wait=True)
                 hand_out(block, wait=True)
 
     each(chips - 1, lambda i: to_chip(i).wait_send())
@@ -303,7 +317,7 @@
             pltpu.VMEM((n, orbitals, width), BF16),
             pltpu.VMEM((n, orbitals, size), BF16),
             pltpu.VMEM((width, size) if width != rows else (8, 128), F32),
-            dma, dma((ring, 2)), dma((ring,)), dma((2, 4)), dma((2, 4)), dma((2,)), dma((2,)),
+            dma, dma((ring, 2, 2)), dma((ring, 2)), dma((2, 4)), dma((2, 4)), dma((2,)), dma((2,)),
             dma((ring, n // ring)), dma((n,)), dma((n // 2,)), dma((n,)), dma((n,)),
         ],
         compiler_params=pltpu.CompilerParams(

time: 45.4 us -> 44.8 us (0.987)
  Pallas kernels: 41.4 us -> 40.8 us
    pallas_call x1, Pallas kernels: 41.4 us -> 40.8 us  [on_device(): pl.pallas_call(functools.partial(kernel, n, ring), out_shape=jax.ShapeDty...]
where the time goes in v4:
time: 44.8 us; the launch traced here: 44.6 us
  Pallas kernels  40.8 us (91%)
  local copies, waits for them, and re-layouts  3.16 us (7%)
  between operations  0.68 us (2%)
    pallas_call x1, Pallas kernels, on_device(): pl.pallas_call(functools.partial(kernel, n, ring), out_shape=jax.ShapeDty...  40.8 us
    unnamed x3, local copies, waits for them, and re-layouts  2.52 us

profile of v4, /device:TPU:7, one launch (start us, length us, event | category | flops | bytes accessed | tf_op | source)
XLA Modules:
  0.0 44.6 jit_solution(2494897733333441492)
XLA Ops:
  0.7 0.0 copy-start
  0.7 0.6 %copy-done = s32[1,2,1]{1,2,0:T(1,128)S(1)} copy-done((s32[1,2,1]{1,2,0:T(1,128)S(1)}, s32[1,2,1]{1,2,0:T(1,128)}, u32[]{:S(2)}) %copy-start) | copy-done | bytes 32
  1.3 0.6 %copy.4.plan_ref = s32[2,1]{1,0:T(2,128)} copy(s32[2,1]{0,1:T(1,128)S(1)} %bitcast.7) | data formatting | bytes 16 | tf_op jit(solution)/shard_map/reshape | solution.py:326
  2.0 40.8 %shard_map.37 = f32[256,512]{1,0:T(8,128)} custom-call(bf16[200,512]{1,0:T(8,128)(2,1)} %bitcast.6, bf16[1,1]{1,0:T(2,128)(2,1)} %bitcast.5.amp_ref, s32[2,1]{1,0:T(2,128)} %copy.4.plan_ref), custom_call_target="tpu_custom_call" | custom-call | tf_op jit(solution)/shard_map/pallas_call | solution.py:304
  42.8 1.9 %copy.7 = f32[256,512]{1,0:T(8,128)} copy(f32[256,512]{1,0:T(8,128)} %shard_map.37) | data formatting | bytes 1048576
Async XLA Ops:
  0.7 0.7 %copy-start = (s32[1,2,1]{1,2,0:T(1,128)S(1)}, s32[1,2,1]{1,2,0:T(1,128)}, u32[]{:S(2)}) copy-start(s32[1,2,1]{1,2,0:T(1,128)} %param.5) | copy-start | bytes 28
